TPU v7x, 256 devices: a whole 4x4x8 slice. The times are simulated.
256 devices in a mesh: context: 32 (over x, z), mp: 8 (over y, core).
Axes of the slice: x: 4, y: 4, z: 8, core: 2. Of those that a mesh axis runs over, the one named last changes fastest.
Arguments:
- queries: bfloat16 [32768, 2048], P('context', 'mp'), may hold values from -32 to 32
- keys: bfloat16 [32768, 1024], P('context', 'mp'), may hold values from -32 to 32
- values: bfloat16 [32768, 1024], P('context', 'mp'), may hold values from -6 to 6
- out_grad: bfloat16 [32768, 5376], P(('context', 'mp')), may hold values from -24 to 24
- out_weight: bfloat16 [5376, 2048], P(None, 'mp'), may hold values from -0.125 to 0.125
Outputs:
- query_grad: bfloat16 [32768, 2048], P('context', 'mp')
- key_grad: bfloat16 [32768, 1024], P('context', 'mp')
- value_grad: bfloat16 [32768, 1024], P('context', 'mp')
- weight_grad: bfloat16 [5376, 2048], P('context', 'mp')
All inputs are finite; a program needn't handle non-finite values.
Results may differ from a plain program's by a relative error of at most 0.02.
Values may be sent and summed in bfloat16 or wider, within the bound.
A program may use at most 128 MiB of HBM per device.

v0:
```python
import jax
import jax.numpy as jnp
from jax import lax
from jax.sharding import PartitionSpec as P

HEAD_SIZE = 128
WINDOW_KEYS = 512
SCALE = 168.0 ** (-0.5)
NEG = -1e30


def shifted(x, axis, by):
    devices = lax.axis_size(axis)
    pairs = [(i, i + by) for i in range(devices) if 0 <= i + by < devices]
    return lax.ppermute(x, axis, pairs)


def band_grads(query_rows_block, key_rows_block, value_rows_block, output_grad_rows, key_start):
    rows = query_rows_block.shape[0]
    span = key_rows_block.shape[0]
    scores = (
        jnp.einsum(
            "qhgd,khd->hgqk", query_rows_block, key_rows_block, preferred_element_type=jnp.float32
        )
        * SCALE
    )
    qpos = jnp.arange(rows, dtype=jnp.int32)[:, None]
    kpos = jnp.arange(span, dtype=jnp.int32)[None, :]
    allowed = (kpos > qpos) & (kpos <= qpos + (span - rows)) & (kpos + key_start >= 0)
    scores = jnp.where(allowed, scores, NEG)
    top = jnp.max(scores, axis=-1, keepdims=True)
    weights = jnp.exp(scores - top)
    prob = weights / jnp.sum(weights, axis=-1, keepdims=True)
    prob_b = prob.astype(jnp.bfloat16)
    attn = jnp.einsum(
        "hgqk,khd->qhgd", prob_b, value_rows_block, preferred_element_type=jnp.float32
    ).astype(jnp.bfloat16)
    delta = jnp.sum(output_grad_rows.astype(jnp.float32) * attn.astype(jnp.float32), axis=-1)
    delta = jnp.transpose(delta, (1, 2, 0))[..., None]
    dprob = jnp.einsum(
        "qhgd,khd->hgqk", output_grad_rows, value_rows_block, preferred_element_type=jnp.float32
    )
    dscore = (prob * (dprob - delta) * SCALE).astype(jnp.bfloat16)
    dq = jnp.einsum("hgqk,khd->qhgd", dscore, key_rows_block, preferred_element_type=jnp.float32)
    key_gradient = jnp.einsum(
        "hgqk,qhgd->khd", dscore, query_rows_block, preferred_element_type=jnp.float32
    )
    value_gradient = jnp.einsum(
        "hgqk,qhgd->khd", prob_b, output_grad_rows, preferred_element_type=jnp.float32
    )
    return (dq, attn, key_gradient, value_gradient)


def shards(queries, keys, values, out_grad, out_weight):
    shard = queries.shape[0]
    kv_local = keys.shape[1] // HEAD_SIZE
    q_local = queries.shape[1] // HEAD_SIZE
    query_group = q_local // kv_local
    block_index = WINDOW_KEYS // 2
    root = lax.axis_index("context") * shard - WINDOW_KEYS
    prev_keys, prev_values = shifted((keys, values), "context", 1)
    prev_keys = prev_keys[shard - WINDOW_KEYS :]
    prev_values = prev_values[shard - WINDOW_KEYS :]
    key_buf = jnp.concatenate([prev_keys, keys], 0)
    value_buf = jnp.concatenate([prev_values, values], 0)
    grad_full = lax.all_gather(out_grad, "mp", axis=0, tiled=True)
    output_gradient = jnp.dot(grad_full, out_weight, preferred_element_type=jnp.float32).astype(
        jnp.bfloat16
    )

    def step(index, carry):
        dq_all, attn_all, key_gradient_total, value_gradient_total = carry
        start_position = index * block_index
        query_rows_block = lax.dynamic_slice_in_dim(
            queries, start_position, block_index, 0
        ).reshape(block_index, kv_local, query_group, HEAD_SIZE)
        output_grad_rows = lax.dynamic_slice_in_dim(
            output_gradient, start_position, block_index, 0
        ).reshape(block_index, kv_local, query_group, HEAD_SIZE)
        key_rows_block = lax.dynamic_slice_in_dim(
            key_buf, start_position, WINDOW_KEYS + block_index, 0
        ).reshape(WINDOW_KEYS + block_index, kv_local, HEAD_SIZE)
        value_rows_block = lax.dynamic_slice_in_dim(
            value_buf, start_position, WINDOW_KEYS + block_index, 0
        ).reshape(WINDOW_KEYS + block_index, kv_local, HEAD_SIZE)
        dq, attn, key_gradient, value_gradient = band_grads(
            query_rows_block,
            key_rows_block,
            value_rows_block,
            output_grad_rows,
            root + start_position,
        )
        dq_all = lax.dynamic_update_slice_in_dim(
            dq_all, dq.reshape(block_index, q_local * HEAD_SIZE), start_position, 0
        )
        attn_all = lax.dynamic_update_slice_in_dim(
            attn_all, attn.reshape(block_index, q_local * HEAD_SIZE), start_position, 0
        )
        earlier_keys = lax.dynamic_slice_in_dim(
            key_gradient_total, start_position, WINDOW_KEYS + block_index, 0
        )
        earlier_values = lax.dynamic_slice_in_dim(
            value_gradient_total, start_position, WINDOW_KEYS + block_index, 0
        )
        key_gradient_total = lax.dynamic_update_slice_in_dim(
            key_gradient_total,
            earlier_keys + key_gradient.reshape(WINDOW_KEYS + block_index, kv_local * HEAD_SIZE),
            start_position,
            0,
        )
        value_gradient_total = lax.dynamic_update_slice_in_dim(
            value_gradient_total,
            earlier_values
            + value_gradient.reshape(WINDOW_KEYS + block_index, kv_local * HEAD_SIZE),
            start_position,
            0,
        )
        return (dq_all, attn_all, key_gradient_total, value_gradient_total)

    start_state = (
        jnp.zeros((shard, q_local * HEAD_SIZE), jnp.float32),
        jnp.zeros((shard, q_local * HEAD_SIZE), jnp.bfloat16),
        jnp.zeros((WINDOW_KEYS + shard, kv_local * HEAD_SIZE), jnp.float32),
        jnp.zeros((WINDOW_KEYS + shard, kv_local * HEAD_SIZE), jnp.float32),
    )
    dq_all, attn_all, key_gradient_total, value_gradient_total = lax.fori_loop(
        0, shard // block_index, step, start_state
    )
    back_keys, back_values = (
        shifted(key_gradient_total[:WINDOW_KEYS].astype(jnp.bfloat16), "context", -1).astype(
            jnp.float32
        ),
        shifted(value_gradient_total[:WINDOW_KEYS].astype(jnp.bfloat16), "context", -1).astype(
            jnp.float32
        ),
    )
    own_keys = key_gradient_total[WINDOW_KEYS:]
    own_values = value_gradient_total[WINDOW_KEYS:]
    key_grad = jnp.concatenate(
        [own_keys[: shard - WINDOW_KEYS], own_keys[shard - WINDOW_KEYS :] + back_keys], 0
    ).astype(jnp.bfloat16)
    value_grad = jnp.concatenate(
        [own_values[: shard - WINDOW_KEYS], own_values[shard - WINDOW_KEYS :] + back_values], 0
    ).astype(jnp.bfloat16)
    query_grad = dq_all.astype(jnp.bfloat16)
    weight_grad = lax.psum_scatter(
        lax.dot_general(
            grad_full, attn_all, (((0,), (0,)), ((), ())), preferred_element_type=jnp.float32
        ),
        "context",
        scatter_dimension=0,
        tiled=True,
    ).astype(jnp.bfloat16)
    return (query_grad, key_grad, value_grad, weight_grad)


def solution(mesh):
    return jax.shard_map(
        shards,
        mesh=mesh,
        in_specs=(
            P("context", "mp"),
            P("context", "mp"),
            P("context", "mp"),
            P(("context", "mp"), None),
            P(None, "mp"),
        ),
        out_specs=(P("context", "mp"), P("context", "mp"), P("context", "mp"), P("context", "mp")),
        check_vma=False,
    )
```

profile of v0, /device:TPU:8, one launch (start us, length us, event | category | flops | bytes accessed | tf_op | source)
XLA Modules:
  0.0 475.2 jit_solution(9497821260364624964)
XLA Ops:
  8.0 4.7 collective-permute-start
  12.7 3.1 collective-permute-start.1
  15.8 3.2 collective-permute-done
  19.9 3.6 collective-permute-done.1
  25.0 50.4 %all-gather.2.cloned.1.call-done = bf16[1024,5376]{1,0:T(8,128)(2,1)} async-done(((bf16[128,5376]{1,0:T(8,128)(2,1)}), bf16[1024,5376]{1,0:T(8,128)(2,1)}) %all-gather.2.cloned.1.call-update) | async-done | bytes 11010064 | tf_op jit(solution)/shard_map/all_gather | solution.py:66
  75.4 7.9 %convolution_convert_fusion.1 = bf16[1024,256]{1,0:T(8,128)(2,1)} fusion(bf16[1024,5376]{1,0:T(8,128)(2,1)} %all-gather.2.cloned.1.call-done, bf16[5376,256]{1,0:T(8,128)(2,1)S(1)} %copy-done), kind=kOutput, calls=%fused_computation.47 | convolution fusion | flops 2818834432 | bytes 14286848 | tf_op jit(solution)/shard_map/dot_general | solution.py:67
  86.9 136.2 %while.19 = (s32[]{:T(128)}, bf16[1024,256]{1,0:T(8,128)(2,1)}, bf16[1024,256]{0,1:T(8,128)(2,1)}, f32[1536,128]{1,0:T(8,128)}, f32[1536,128]{1,0:T(8,128)}, /*i...) while((s32[]{:T(128)}, bf16[1024,256]{1,0:T(8,128)(2,1)}, ...), condition=%wide.region_4.5_spmd, body=%wide.region_0.4_spmd.sunk | while | flops 610795776 | bytes 35936128 | solution.py:126
  95.9 3.1 fusion.72
  101.6 2.4 fusion.75
  109.6 2.2 fusion.74
  129.9 3.1 fusion.72
  135.7 2.4 fusion.75
  143.7 2.2 fusion.74
  164.0 3.1 fusion.72
  169.7 2.4 fusion.75
  177.7 2.2 fusion.74
  198.0 3.1 fusion.72
  203.8 2.4 fusion.75
  211.8 2.2 fusion.74
  215.9 2.1 constant_dynamic-update-slice_fusion.9
  223.2 9.7 %convolution_bitcast_fusion.2 = f32[5376,256]{0,1:T(8,128)} fusion(bf16[1024,256]{0,1:T(8,128)(2,1)} %get-tuple-element.179, bf16[1024,5376]{1,0:T(8,128)(2,1)} %all-gather.2.cloned.1.call-done), kind=kOutput, calls=%fused_computation.46 | convolution fusion | flops 2818572288 | bytes 17039360 | tf_op jit(solution)/shard_map/dot_general | solution.py:147
  232.9 6.1 %copy.66 = f32[5376,256]{1,0:T(8,128)} copy(f32[5376,256]{0,1:T(8,128)} %convolution_bitcast_fusion.2) | data formatting | bytes 11010048
  242.9 5.5 %collective-permute-done.3 = bf16[512,128]{1,0:T(8,128)(2,1)S(1)} collective-permute-done((bf16[512,128]{1,0:T(8,128)(2,1)S(1)}, bf16[512,128]{1,0:T(8,128)(2,1)S(1)}, u32[]{:S(2)}, u32[]{:S(2)}) %collective-permute-start.3) | collective-permute-done | bytes 131104 | tf_op jit(solution)/shard_map/ppermute | solution.py:15
  251.3 215.3 %reduce-scatter.4.cloned.1.call-done = f32[168,256]{1,0:T(8,128)} async-done(((f32[5376,256]{1,0:T(8,128)}), f32[168,256]{1,0:T(8,128)}) %reduce-scatter.4.cloned.1.call-update) | async-done | bytes 172048
  (154 shorter events, 118.4 us)
Async XLA Ops:
  7.2 68.2 %copy-start = (bf16[5376,256]{1,0:T(8,128)(2,1)S(1)}, bf16[5376,256]{1,0:T(8,128)(2,1)}, u32[]{:S(2)}) copy-start(bf16[5376,256]{1,0:T(8,128)(2,1)} %param.11) | copy-start | bytes 8257540
  7.2 16.3 %copy-start.7 = (bf16[1024,128]{1,0:T(8,128)(2,1)S(1)}, bf16[1024,128]{1,0:T(8,128)(2,1)}, u32[]{:S(2)}) copy-start(bf16[1024,128]{1,0:T(8,128)(2,1)} %param.8) | copy-start | bytes 786436
  7.2 17.0 %copy-start.8 = (bf16[1024,128]{1,0:T(8,128)(2,1)S(1)}, bf16[1024,128]{1,0:T(8,128)(2,1)}, u32[]{:S(2)}) copy-start(bf16[1024,128]{1,0:T(8,128)(2,1)} %param.9) | copy-start | bytes 786436
  7.2 68.2 %all-gather.2.cloned.1.call-start = ((), (), s32[]{:S(2)}) async-start(), calls=%async_computation.1 | async-start | bytes 12386304 | tf_op jit(solution)/shard_map/all_gather | solution.py:66
  7.9 458.7 %reduce-scatter.4.cloned.1.call-start = ((), (), s32[]{:S(2)}) async-start(), calls=%async_computation.2 | async-start | bytes 5677056
  8.0 11.0 %collective-permute-start = (bf16[1024,128]{1,0:T(8,128)(2,1)}, bf16[1024,128]{1,0:T(8,128)(2,1)}, u32[]{:S(2)}, u32[]{:S(2)}) collective-permute-start(bf16[1024,128]{1,0:T(8,128)(2,1)} %param.8), channel_id=1, source_target_pairs={{0,8},{8,16},{16,24},{24,32},{32,40},{40,48},{48,56},{56,64},{64,7... | collective-permute-start | bytes 786440 | tf_op jit(solution)/shard_map/ppermute | solution.py:15
  12.7 10.8 %collective-permute-start.1 = (bf16[1024,128]{1,0:T(8,128)(2,1)}, bf16[1024,128]{1,0:T(8,128)(2,1)S(1)}, u32[]{:S(2)}, u32[]{:S(2)}) collective-permute-start(bf16[1024,128]{1,0:T(8,128)(2,1)} %param.9), channel_id=1, source_target_pairs={{0,8},{8,16},{16,24},{24,32},{32,40},{40,48},{48,56},{56,64},{64,7... | collective-permute-start | bytes 786440 | tf_op jit(solution)/shard_map/ppermute | solution.py:15
  87.9 1.6 copy-start.3
  89.5 1.2 copy-start.1
  95.9 3.1 copy-start.4
  111.8 4.0 copy-start.2
  122.0 1.6 copy-start.3
  129.9 3.1 copy-start.4
  145.9 4.0 copy-start.2
  156.1 1.6 copy-start.3
  157.6 1.2 copy-start.1
  164.0 3.1 copy-start.4
  179.9 4.0 copy-start.2
  190.1 1.6 copy-start.3
  198.0 3.1 copy-start.4
  213.9 4.1 copy-start.2
  239.0 2.5 copy-start.5
  240.2 8.2 %collective-permute-start.3 = (bf16[512,128]{1,0:T(8,128)(2,1)S(1)}, bf16[512,128]{1,0:T(8,128)(2,1)S(1)}, u32[]{:S(2)}, u32[]{:S(2)}) collective-permute-start(bf16[512,128]{1,0:T(8,128)(2,1)S(1)} %get-tuple-element.249), channel_id=1, source_target_pairs={{8,0},{16,8},{24,16},{32,24},{40,32},{48,40},{56,48},{64,56},{72,6... | collective-permute-start | bytes 393224 | tf_op jit(solution)/shard_map/ppermute | solution.py:15
  241.6 9.0 %collective-permute-start.2 = (bf16[512,128]{1,0:T(8,128)(2,1)S(1)}, bf16[512,128]{1,0:T(8,128)(2,1)S(1)}, u32[]{:S(2)}, u32[]{:S(2)}) collective-permute-start(bf16[512,128]{1,0:T(8,128)(2,1)S(1)} %get-tuple-element.251), channel_id=1, source_target_pairs={{8,0},{16,8},{24,16},{32,24},{40,32},{48,40},{56,48},{64,56},{72,6... | collective-permute-start | bytes 393224 | tf_op jit(solution)/shard_map/ppermute | solution.py:15
  (3 other events, 3.5 us)
Sparse Core Ops, SparseCore 0:
  9.9 65.4 all-gather.1
  239.1 227.4 reduce-scatter.3
where the time goes:
time: 477 us; the launch traced here: 475 us
  waiting for transfers between devices  280 us (59%)
  local copies, waits for them, and re-layouts  95.5 us (20%)
  matrix products  68.8 us (14%)
  between operations  14.2 us (3%)
  starting transfers between devices  10.5 us (2%)
  other arithmetic  5.89 us (1%)
    unnamed x3, waiting for transfers between devices  216 us
    all_gather x1, waiting for transfers between devices, shards(): grad_full = lax.all_gather(out_grad, 'mp', axis=0, tiled=True)  50.4 us
    dynamic_update_slice x8, local copies, waits for them, and re-layouts, step(): lax.dynamic_update_slice_in_dim(value_gradient_total, earlier_values + va...  16.1 us
    dynamic_slice x8, local copies, waits for them, and re-layouts, step(): lax.dynamic_slice_in_dim(value_gradient_total, start_position, WINDOW_KEY...  14.7 us
    ppermute x4, waiting for transfers between devices, shifted(): return lax.ppermute(x, axis, pairs)  13.6 us
    dynamic_slice x8, local copies, waits for them, and re-layouts, step(): lax.dynamic_slice_in_dim(output_gradient, start_position, block_index, 0)  12.9 us
    dot_general x4, matrix products, band_grads(): jnp.einsum('qhgd,khd->hgqk', output_grad_rows, value_rows_block, preferre...  12.2 us
    dynamic_slice x8, local copies, waits for them, and re-layouts, step(): lax.dynamic_slice_in_dim(key_gradient_total, start_position, WINDOW_KEYS...  10.7 us
  transfers between devices with their start and end apart: 6, of which 6 were waited for; matrix products, arithmetic and copies ran while one was open for 1% of the time, Pallas kernels for 0%

commit v1 on v0

--- a/solution.py
+++ b/solution.py
@@ -63,7 +63,11 @@
     prev_values = prev_values[shard - WINDOW_KEYS :]
     key_buf = jnp.concatenate([prev_keys, keys], 0)
     value_buf = jnp.concatenate([prev_values, values], 0)
-    grad_full = lax.all_gather(out_grad, "mp", axis=0, tiled=True)
+    _number_kinds = lambda u_in, at_axis: jnp.concatenate(
+        lax.all_to_all(jnp.stack([u_in for _ in range(lax.axis_size("mp"))], axis=0), "mp", 0, 0),
+        at_axis,
+    )
+    grad_full = _number_kinds(out_grad, 0)
     output_gradient = jnp.dot(grad_full, out_weight, preferred_element_type=jnp.float32).astype(
         jnp.bfloat16
     )

time: 477 us -> 543 us (1.14)
  waiting for transfers between devices: 280 us -> 334 us
  local copies, waits for them, and re-layouts: 95.5 us -> 102 us
    all_to_all x0 -> x1, waiting for transfers between devices: none -> 106 us  [shards(): lax.all_to_all(jnp.stack([u_in for _ in range(lax.axis_size('mp'))], axis...]
    all_gather x1 -> x0, waiting for transfers between devices: 50.4 us -> none  [shards(): grad_full = lax.all_gather(out_grad, 'mp', axis=0, tiled=True)]
    all_to_all x0 -> x1, starting transfers between devices: none -> 7.4 us  [shards(): lax.all_to_all(jnp.stack([u_in for _ in range(lax.axis_size('mp'))], axis...]
    another operation x2 -> x3, local copies, waits for them, and re-layouts: 1.89 us -> 8.12 us  [the longest x1 6.22 us: shards(): jnp.stack([u_in for _ in range(lax.axis_size('mp'))], axis=0)]
    unnamed x3 -> x2, waiting for transfers between devices: 216 us -> 215 us
where the time goes in v1:
time: 543 us; the launch traced here: 541 us
  waiting for transfers between devices  334 us (62%)
  local copies, waits for them, and re-layouts  102 us (19%)
  matrix products  68.8 us (13%)
  starting transfers between devices  15.9 us (3%)
  between operations  14.1 us (3%)
  other arithmetic  5.94 us (1%)
    unnamed x2, waiting for transfers between devices  215 us
    all_to_all x1, waiting for transfers between devices, shards(): lax.all_to_all(jnp.stack([u_in for _ in range(lax.axis_size('mp'))], axis...  106 us
    dynamic_update_slice x8, local copies, waits for them, and re-layouts, step(): lax.dynamic_update_slice_in_dim(value_gradient_total, earlier_values + va...  16.1 us
    dynamic_slice x8, local copies, waits for them, and re-layouts, step(): lax.dynamic_slice_in_dim(value_gradient_total, start_position, WINDOW_KEY...  14.7 us
    ppermute x4, waiting for transfers between devices, shifted(): return lax.ppermute(x, axis, pairs)  13 us
    dynamic_slice x8, local copies, waits for them, and re-layouts, step(): lax.dynamic_slice_in_dim(output_gradient, start_position, block_index, 0)  12.9 us
    dot_general x4, matrix products, band_grads(): jnp.einsum('qhgd,khd->hgqk', output_grad_rows, value_rows_block, preferre...  12.2 us
  transfers between devices with their start and end apart: 6, of which 6 were waited for; matrix products, arithmetic and copies ran while one was open for 1% of the time, Pallas kernels for 0%

profile of v1, /device:TPU:8, one launch (start us, length us, event | category | flops | bytes accessed | tf_op | source)
XLA Modules:
  0.0 541.1 jit_solution(4988331626312794190)
XLA Ops:
  7.2 6.2 %stack.2 = bf16[8,128,5376]{2,1,0:T(8,128)(2,1)} broadcast(bf16[128,5376]{1,0:T(8,128)(2,1)} %param.10), dimensions={1,2} | broadcast | bytes 12386304 | tf_op jit(solution)/shard_map/stack | solution.py:67
  13.4 7.4 %all-to-all-start = ((bf16[8,128,5376]{2,1,0:T(8,128)(2,1)}), bf16[8,128,5376]{2,1,0:T(8,128)(2,1)}, u32[]{:S(2)}, u32[]{:S(2)}) async-start(bf16[8,128,5376]{2,1,0:T(8,128)(2,1)} %stack.2), calls=%async_computation | async-start | bytes 22020096 | tf_op jit(solution)/shard_map/all_to_all | solution.py:67
  20.8 2.8 collective-permute-start
  23.6 3.1 collective-permute-start.1
  26.8 2.8 collective-permute-done
  30.5 3.9 collective-permute-done.1
  36.0 106.2 %all-to-all-done = bf16[8,128,5376]{2,1,0:T(8,128)(2,1)} async-done(((bf16[8,128,5376]{2,1,0:T(8,128)(2,1)}), bf16[8,128,5376]{2,1,0:T(8,128)(2,1)}, u32[]{:S(2)}, u32[]{:S(2)}) %all-to-all-start) | async-done | bytes 11010080 | tf_op jit(solution)/shard_map/all_to_all | solution.py:67
  142.2 7.9 %convolution_convert_fusion.1 = bf16[1024,256]{1,0:T(8,128)(2,1)} fusion(bf16[1024,5376]{1,0:T(8,128)(2,1)} %bitcast.31, bf16[5376,256]{1,0:T(8,128)(2,1)S(1)} %copy-done), kind=kOutput, calls=%fused_computation.47 | convolution fusion | flops 2818834432 | bytes 14286848 | tf_op jit(solution)/shard_map/dot_general | solution.py:71
  153.7 136.3 %while.19 = (s32[]{:T(128)}, bf16[1024,256]{1,0:T(8,128)(2,1)}, bf16[1024,256]{0,1:T(8,128)(2,1)}, f32[1536,128]{1,0:T(8,128)}, f32[1536,128]{1,0:T(8,128)}, /*i...) while((s32[]{:T(128)}, bf16[1024,256]{1,0:T(8,128)(2,1)}, ...), condition=%wide.region_4.5_spmd, body=%wide.region_0.4_spmd.sunk | while | flops 610795776 | bytes 35936128 | solution.py:130
  162.6 3.1 fusion.72
  168.4 2.4 fusion.75
  196.7 3.1 fusion.72
  202.4 2.4 fusion.75
  210.4 2.2 fusion.74
  230.8 3.1 fusion.72
  236.5 2.4 fusion.75
  244.5 2.2 fusion.74
  264.8 3.1 fusion.72
  270.6 2.4 fusion.75
  278.6 2.2 fusion.74
  290.0 9.7 %convolution_bitcast_fusion.2 = f32[5376,256]{0,1:T(8,128)} fusion(bf16[1024,256]{0,1:T(8,128)(2,1)} %get-tuple-element.179, bf16[1024,5376]{1,0:T(8,128)(2,1)} %bitcast.31), kind=kOutput, calls=%fused_computation.46 | convolution fusion | flops 2818572288 | bytes 17039360 | tf_op jit(solution)/shard_map/dot_general | solution.py:151
  299.7 6.1 %copy.66 = f32[5376,256]{1,0:T(8,128)} copy(f32[5376,256]{0,1:T(8,128)} %convolution_bitcast_fusion.2) | data formatting | bytes 11010048
  309.7 5.1 collective-permute-done.3
  317.5 215.0 %reduce-scatter.4.cloned.1.call-done = f32[168,256]{1,0:T(8,128)} async-done(((f32[5376,256]{1,0:T(8,128)}), f32[168,256]{1,0:T(8,128)}) %reduce-scatter.4.cloned.1.call-update) | async-done | bytes 172048
  (154 shorter events, 121.8 us)
Async XLA Ops:
  7.2 135.0 %copy-start = (bf16[5376,256]{1,0:T(8,128)(2,1)S(1)}, bf16[5376,256]{1,0:T(8,128)(2,1)}, u32[]{:S(2)}) copy-start(bf16[5376,256]{1,0:T(8,128)(2,1)} %param.11) | copy-start | bytes 8257540
  13.4 7.4 %copy-start.7 = (bf16[1024,128]{1,0:T(8,128)(2,1)S(1)}, bf16[1024,128]{1,0:T(8,128)(2,1)}, u32[]{:S(2)}) copy-start(bf16[1024,128]{1,0:T(8,128)(2,1)} %param.8) | copy-start | bytes 786436
  13.4 10.2 %copy-start.8 = (bf16[1024,128]{1,0:T(8,128)(2,1)S(1)}, bf16[1024,128]{1,0:T(8,128)(2,1)}, u32[]{:S(2)}) copy-start(bf16[1024,128]{1,0:T(8,128)(2,1)} %param.9) | copy-start | bytes 786436
  13.4 128.8 %all-to-all-start = ((bf16[8,128,5376]{2,1,0:T(8,128)(2,1)}), bf16[8,128,5376]{2,1,0:T(8,128)(2,1)}, u32[]{:S(2)}, u32[]{:S(2)}) async-start(bf16[8,128,5376]{2,1,0:T(8,128)(2,1)} %stack.2), calls=%async_computation | async-start | bytes 22020096 | tf_op jit(solution)/shard_map/all_to_all | solution.py:67
  20.8 511.7 %reduce-scatter.4.cloned.1.call-start = ((), (), s32[]{:S(2)}) async-start(), calls=%async_computation.2 | async-start | bytes 5677056
  20.8 8.7 %collective-permute-start = (bf16[1024,128]{1,0:T(8,128)(2,1)S(1)}, bf16[1024,128]{1,0:T(8,128)(2,1)}, u32[]{:S(2)}, u32[]{:S(2)}) collective-permute-start(bf16[1024,128]{1,0:T(8,128)(2,1)S(1)} %copy-done.7), channel_id=1, source_target_pairs={{0,8},{8,16},{16,24},{24,32},{32,40},{40,48},{48,56},{56,64},{64,7... | collective-permute-start | bytes 786440 | tf_op jit(solution)/shard_map/ppermute | solution.py:15
  23.6 10.8 %collective-permute-start.1 = (bf16[1024,128]{1,0:T(8,128)(2,1)S(1)}, bf16[1024,128]{1,0:T(8,128)(2,1)S(1)}, u32[]{:S(2)}, u32[]{:S(2)}) collective-permute-start(bf16[1024,128]{1,0:T(8,128)(2,1)S(1)} %copy-done.8), channel_id=1, source_target_pairs={{0,8},{8,16},{16,24},{24,32},{32,40},{40,48},{48,56},{56,64},{64,7... | collective-permute-start | bytes 786440 | tf_op jit(solution)/shard_map/ppermute | solution.py:15
  154.7 1.6 copy-start.3
  156.3 1.2 copy-start.1
  162.6 3.1 copy-start.4
  178.6 4.0 copy-start.2
  188.8 1.6 copy-start.3
  190.3 1.2 copy-start.1
  196.7 3.1 copy-start.4
  212.6 4.0 copy-start.2
  222.9 1.6 copy-start.3
  230.8 3.1 copy-start.4
  246.7 4.0 copy-start.2
  256.9 1.6 copy-start.3
  264.8 3.1 copy-start.4
  280.8 4.1 copy-start.2
  305.8 2.5 copy-start.5
  307.0 7.8 %collective-permute-start.3 = (bf16[512,128]{1,0:T(8,128)(2,1)S(1)}, bf16[512,128]{1,0:T(8,128)(2,1)S(1)}, u32[]{:S(2)}, u32[]{:S(2)}) collective-permute-start(bf16[512,128]{1,0:T(8,128)(2,1)S(1)} %get-tuple-element.249), channel_id=1, source_target_pairs={{8,0},{16,8},{24,16},{32,24},{40,32},{48,40},{56,48},{64,56},{72,6... | collective-permute-start | bytes 393224 | tf_op jit(solution)/shard_map/ppermute | solution.py:15
  308.4 8.4 %collective-permute-start.2 = (bf16[512,128]{1,0:T(8,128)(2,1)S(1)}, bf16[512,128]{1,0:T(8,128)(2,1)S(1)}, u32[]{:S(2)}, u32[]{:S(2)}) collective-permute-start(bf16[512,128]{1,0:T(8,128)(2,1)S(1)} %get-tuple-element.251), channel_id=1, source_target_pairs={{8,0},{16,8},{24,16},{32,24},{40,32},{48,40},{56,48},{64,56},{72,6... | collective-permute-start | bytes 393224 | tf_op jit(solution)/shard_map/ppermute | solution.py:15
  (3 other events, 3.5 us)
Sparse Core Ops, SparseCore 0:
  306.0 226.5 reduce-scatter.3
